TPU v7x, 32 devices: a whole 2x2x4 slice. The times are simulated.
32 devices in a mesh: parts: 2 (over y), fsdp: 8 (over z, x), rep: 2 (over core).
Axes of the slice: x: 2, y: 2, z: 4, core: 2. Of those that a mesh axis runs over, the one named last changes fastest.
Arguments:
- tokens: bfloat16 [2, 4096, 5120], P('rep', ('parts', 'fsdp')), parts along dimension 1, may hold values from -6 to 6
- cotangent: bfloat16 [2, 4096, 8], P('rep', ('parts', 'fsdp')), parts along dimension 1, may hold values from -0.1875 to 0.1875
- params: float32 [16, 5120], P(('parts', 'fsdp')), parts along dimension 0, may hold values from -0.078125 to 0.078125
- momentum: float32 [2, 16, 5120], P('rep', ('parts', 'fsdp')), parts along dimension 1, may hold values from -6 to 6
- indices: int32 [2, 16, 40, 16], P('rep', ('parts', 'fsdp')), parts along dimension 1, may hold values from 0 to 127, all different within a row
Outputs:
- new_params: float32 [16, 5120], P(('parts', 'fsdp')), parts along dimension 0
- new_momentum: float32 [2, 16, 5120], P('rep', ('parts', 'fsdp')), parts along dimension 1
There are 2 independent parts, one for each index of `parts`. A program takes and returns all parts, laid end to end along the dimension named above; each array names one. Nothing has to cross between parts.
Inputs may be any that keep to these rules, and one draw needn't show every extreme that they name: Within each block the 16 indices are distinct.
All inputs are finite; a program needn't handle non-finite values.
Results may differ from a plain program's by a relative error of at most 0.0003.
Values sent between devices are 32-bit elements; how exact they have to be, the bound alone decides.
No kernel may reach another device: no remote copies, remote signals or barrier semaphores. Data moves between devices by JAX's collectives and lax.ppermute only.
A program may use at most 64 MiB of HBM per device.

v0:
```python
import jax
import jax.numpy as jnp
from jax import lax
from jax.sharding import PartitionSpec as P

SPAN = 128


momentum_decay = 0.9
learn_rate = 0.5


def span_basis(length):
    freq = jnp.arange(length, dtype=jnp.float32)[:, None]
    place = jnp.arange(length, dtype=jnp.float32)[None, :]
    scale = jnp.where(freq == 0.0, jnp.sqrt(1.0 / length), jnp.sqrt(2.0 / length))
    return scale * jnp.cos(jnp.pi * (2.0 * place + 1.0) * freq / (2.0 * length))


def local(tokens, cotangent, params, momentum, indices):
    local_tokens = tokens[0]
    local_cot = cotangent[0]
    width = local_tokens.shape[1]
    blocks_row = width // SPAN
    high = lax.Precision.HIGHEST
    basis = span_basis(SPAN)
    slots = jnp.arange(SPAN, dtype=jnp.int32)
    picks = indices[0]
    selector = (picks[..., None] == slots).astype(jnp.float32)
    gradient = lax.psum_scatter(
        lax.dot_general(
            local_cot, local_tokens, (((0,), (0,)), ((), ())), preferred_element_type=jnp.float32
        ),
        "fsdp",
        scatter_dimension=0,
        tiled=True,
    )
    rows_dev = gradient.shape[0]
    moved = momentum_decay * momentum[0] + gradient
    coeffs = jnp.einsum(
        "rjn,kn->rjk", moved.reshape(rows_dev, blocks_row, SPAN), basis, precision=high
    )
    chosen = jnp.einsum("rjc,rjtc->rjt", coeffs, selector, precision=high)
    sent = jnp.einsum("rjt,rjtc->rjc", chosen, selector, precision=high)
    back = jnp.einsum("rjk,kn->rjn", sent, basis, precision=high).reshape(rows_dev, width)
    kept = moved - back
    values, places = (
        lax.all_gather(chosen[None], "rep", axis=0, tiled=True),
        lax.all_gather(picks[None], "rep", axis=0, tiled=True),
    )
    placed = (places[..., None] == slots).astype(jnp.float32)
    summed = jnp.einsum("arjt,arjtc->rjc", values, placed, precision=high)
    mean_sent = summed / lax.axis_size("rep")
    update = jnp.einsum("rjk,kn->rjn", mean_sent, basis, precision=high).reshape(rows_dev, width)
    return (params - learn_rate * update, kept[None])


def solution(mesh):
    in_specs = (
        P("rep", ("parts", "fsdp"), None),
        P("rep", ("parts", "fsdp"), None),
        P(("parts", "fsdp"), None),
        P("rep", ("parts", "fsdp"), None),
        P("rep", ("parts", "fsdp"), None, None),
    )
    out_specs = (P(("parts", "fsdp"), None), P("rep", ("parts", "fsdp"), None))
    return jax.shard_map(local, mesh=mesh, in_specs=in_specs, out_specs=out_specs, check_vma=False)
```

profile of v0, /device:TPU:0, one launch (start us, length us, event | category | flops | bytes accessed | tf_op | source)
XLA Modules:
  0.0 98.6 jit_solution(9816798639374426935)
XLA Ops:
  7.2 0.0 copy-start
  7.2 0.0 copy-start.4
  7.2 0.0 copy-start.1
  7.2 0.0 copy-start.2
  7.2 0.0 copy-start.3
  7.2 0.0 all-reduce.3.cloned.1.call-start
  7.3 1.7 %copy-done = bf16[1,256,5120]{2,1,0:T(8,128)(2,1)S(1)} copy-done((bf16[1,256,5120]{2,1,0:T(8,128)(2,1)S(1)}, bf16[1,256,5120]{2,1,0:T(8,128)(2,1)}, u32[]{:S(2)}) %copy-start) | copy-done | bytes 2621464
  8.9 1.8 %fusion = f32[8,5120]{1,0:T(8,128)} fusion(bf16[1,256,5120]{2,1,0:T(8,128)(2,1)S(1)} %copy-done, bf16[1,256,8]{1,2,0:T(8,128)(2,1)} %param.6), kind=kOutput, calls=%fused_computation | convolution fusion | flops 20971520 | bytes 2789376 | tf_op jit(solution)/shard_map/dot_general | solution.py:31
  10.7 0.0 all-reduce.3.cloned.1.call-update
  10.8 0.0 copy-done.1
  10.8 0.1 copy.9
  10.9 2.0 %all_gather.7 = s32[2,1,40,16]{2,3,1,0:T(8,128)S(1)} all-gather(s32[1,1,40,16]{2,3,1,0:T(8,128)S(1)} %copy-done.1), channel_id=1, replica_groups=mesh['parts'=2,'fsdp'=8,'rep'=2] {'rep'}, dimensions={0}, use_global_device_ids=true | all-gather | bytes 7680 | tf_op jit(solution)/shard_map/all_gather | solution.py:49
  12.8 0.1 copy.10
  12.9 0.0 copy-done.4
  12.9 0.6 dynamic-slice
  13.5 70.6 %all-reduce.3.cloned.1.call-done = f32[8,5120]{1,0:T(8,128)} async-done(((f32[8,5120]{1,0:T(8,128)}), f32[8,5120]{1,0:T(8,128)}) %all-reduce.3.cloned.1.call-update) | async-done | bytes 163856
  84.1 0.0 copy-done.2
  84.1 1.6 %dynamic-slice_add_fusion = f32[1,5120]{1,0:T(1,128)S(1)} fusion(f32[8,5120]{1,0:T(8,128)} %all-reduce.3.cloned.1.call-done, u32[]{:T(128)} %bitcast.19, f32[1,1,5120]{2,1,0:T(1,128)S(1)} %copy-done.2), kind=kLoop, calls=%fused_computation.23 | loop fusion | flops 10240 | bytes 61444 | tf_op jit(solution)/shard_map/add | solution.py:39
  85.7 0.5 fusion.9
  86.2 0.4 fusion.5
  86.7 0.1 copy.12
  86.7 0.1 copy.16
  86.8 0.4 fusion.4
  87.2 0.4 fusion.8
  87.6 0.6 subtract_bitcast_fusion
  88.3 1.8 %all-gather.1 = f32[2,40,16]{1,2,0:T(8,128)S(1)} all-gather(f32[1,40,16]{1,2,0:T(8,128)S(1)} %bitcast.35), channel_id=2, replica_groups=mesh['parts'=2,'fsdp'=8,'rep'=2] {'rep'}, dimensions={0}, use_global_device_ids=true | all-gather | bytes 7680 | tf_op jit(solution)/shard_map/all_gather | solution.py:48
  90.1 0.1 copy.13
  90.1 0.6 fusion.2
  90.7 0.4 convolution_multiply_fusion
  91.2 0.0 copy-done.3
  91.2 0.6 sub.6
  (1 shorter events, 0.0 us)
Async XLA Ops:
  7.2 1.8 %copy-start = (bf16[1,256,5120]{2,1,0:T(8,128)(2,1)S(1)}, bf16[1,256,5120]{2,1,0:T(8,128)(2,1)}, u32[]{:S(2)}) copy-start(bf16[1,256,5120]{2,1,0:T(8,128)(2,1)} %param.5) | copy-start | bytes 7864324
  7.2 5.7 %copy-start.4 = (u32[32]{0:T(128)S(1)}, u32[32]{0:T(128)}, u32[]{:S(2)}) copy-start(u32[32]{0:T(128)} %constant.28) | copy-start | bytes 388
  7.2 3.6 %copy-start.1 = (s32[1,1,40,16]{2,3,1,0:T(8,128)S(1)}, s32[1,1,40,16]{2,3,1,0:T(8,128)}, u32[]{:S(2)}) copy-start(s32[1,1,40,16]{2,3,1,0:T(8,128)} %param.9) | copy-start | bytes 7684
  7.2 76.9 %copy-start.2 = (f32[1,1,5120]{2,1,0:T(1,128)S(1)}, f32[1,1,5120]{2,1,0:T(1,128)}, u32[]{:S(2)}) copy-start(f32[1,1,5120]{2,1,0:T(1,128)} %param.8) | copy-start | bytes 61444
  7.2 84.0 %copy-start.3 = (f32[1,5120]{1,0:T(1,128)S(1)}, f32[1,5120]{1,0:T(1,128)}, u32[]{:S(2)}) copy-start(f32[1,5120]{1,0:T(1,128)} %param.7) | copy-start | bytes 61444
  7.2 76.9 %all-reduce.3.cloned.1.call-start = ((), (), s32[]{:S(2)}) async-start(), calls=%async_computation | async-start | bytes 327680
Sparse Core Ops, SparseCore 0:
  11.4 72.7 all-reduce.2
where the time goes:
time: 98.9 us; the launch traced here: 98.6 us
  waiting for transfers between devices  70.7 us (71%)
  between operations  14.1 us (14%)
  matrix products  4.54 us (5%)
  blocking collectives  3.76 us (4%)
  other arithmetic  2.87 us (3%)
  local copies, waits for them, and re-layouts  2.65 us (3%)
    unnamed x2, waiting for transfers between devices  70.7 us
    unnamed x11, local copies, waits for them, and re-layouts  2.27 us
  transfers between devices with their start and end apart: 1, of which 1 were waited for; matrix products, arithmetic and copies ran while one was open for 1% of the time, Pallas kernels for 0%

commit v1 on v0

v1 whole, which is shorter than its diff:
```python
import jax
import jax.numpy as jnp
import numpy as np
from jax import lax
from jax.experimental import pallas as pl
from jax.experimental.pallas import tpu as pltpu
from jax.sharding import PartitionSpec as P

SPAN = 128

momentum_decay = 0.9
learn_rate = 0.5


def span_basis(length):
    freq = np.arange(length, dtype=np.float64)[:, None]
    place = np.arange(length, dtype=np.float64)[None, :]
    scale = np.where(freq == 0.0, np.sqrt(1.0 / length), np.sqrt(2.0 / length))
    return scale * np.cos(np.pi * (2.0 * place + 1.0) * freq / (2.0 * length))


def split_factor(matrix):
    high = matrix.astype(jnp.bfloat16)
    low = (matrix - high.astype(np.float64)).astype(jnp.bfloat16)
    return np.block([[high, low], [high, low]])


def split_dot(x, factor):
    high = x.astype(jnp.bfloat16)
    low = (x - high.astype(jnp.float32)).astype(jnp.bfloat16)
    y = jnp.dot(jnp.concatenate([high, low], 1), factor, preferred_element_type=jnp.float32)
    half = y.shape[1] // 2
    return y[:, :half] + y[:, half:]


def select_kernel(count, *refs):
    terms, (momentum, mask, forward, inverse, total, lost) = refs[:count], refs[count:]
    moved = momentum_decay * momentum[...]
    for term in terms:
        moved = moved + term[...]
    coeffs = split_dot(moved, forward[...])
    sent = jnp.where(mask[...] > 0.0, coeffs, 0.0)
    total[...] = moved
    lost[...] = split_dot(sent, inverse[...])


def select(terms, momentum, indices):
    blocks = momentum.size // SPAN
    terms = [t.reshape(blocks, SPAN) for t in terms]
    slots = jnp.arange(SPAN, dtype=jnp.int32)
    mask = jnp.any(indices.reshape(blocks, -1, 1) == slots, 1).astype(jnp.float32)
    basis = span_basis(SPAN)
    shape = jax.ShapeDtypeStruct((blocks, SPAN), jnp.float32)
    vmem = pl.BlockSpec(memory_space=pltpu.VMEM)
    moved, lost = pl.pallas_call(
        lambda *refs: select_kernel(len(terms), *refs),
        out_shape=(shape, shape),
        in_specs=[vmem] * (len(terms) + 4),
        out_specs=(vmem, vmem),
        compiler_params=pltpu.CompilerParams(vmem_limit_bytes=4 << 20),
        name="select",
    )(*terms, momentum.reshape(blocks, SPAN), mask, split_factor(basis.T), split_factor(basis))
    return moved, lost


def staged(n):
    return n in (4, 8, 16)


def send(x, n, reps, offset):
    pairs = [(i * reps + c, (i ^ offset) * reps + (c + 1) % reps) for i in range(n) for c in range(reps)]
    return lax.ppermute(x, ("fsdp", "rep"), pairs)


def near_rows(cot, tok, me, n):
    place = jnp.arange(n, dtype=jnp.int32)
    wanted = (place // (n // 4)) ^ (place % (n // 4) * 4) ^ me
    picked = (wanted[:, None] == place).astype(cot.dtype)
    left = lax.dot_general(picked, cot, (((1,), (1,)), ((), ())), preferred_element_type=jnp.float32)
    left = lax.optimization_barrier(left.astype(cot.dtype).reshape(4, n // 4, -1))
    return lax.dot_general(left, tok, (((2,), (0,)), ((), ())), preferred_element_type=jnp.float32)


def local(tokens, cotangent, params, momentum, indices):
    tok, cot = tokens[0], cotangent[0]
    n, reps = lax.axis_size("fsdp"), lax.axis_size("rep")
    if staged(n) and reps == 2 and params.shape[0] == 1:
        own, *rest = near_rows(cot, tok, lax.axis_index("fsdp"), n)
        arrived = [send(x, n, reps, k) for k, x in enumerate(rest, 1)]
        part = send(own, n, reps, 0)
        for x in arrived:
            part = part + x
        terms = []
        for k in range(n // 4):
            terms.append(send(part[k : k + 1], n, reps, 4 * k))
    else:
        gradient = lax.dot_general(cot, tok, (((0,), (0,)), ((), ())), preferred_element_type=jnp.float32)
        terms = [lax.psum_scatter(gradient, "fsdp", scatter_dimension=0, tiled=True)]
    moved, lost = select(terms, momentum, indices)
    if reps == 2:
        back = lost.reshape(params.shape)
        total = back + send(back, n, reps, 0)
    else:
        total = lax.psum(lost.reshape(params.shape), "rep")
    return params - learn_rate / reps * total, (moved - lost).reshape(momentum.shape)


def solution(mesh):
    in_specs = (
        P("rep", ("parts", "fsdp"), None),
        P("rep", ("parts", "fsdp"), None),
        P(("parts", "fsdp"), None),
        P("rep", ("parts", "fsdp"), None),
        P("rep", ("parts", "fsdp"), None, None),
    )
    out_specs = (P(("parts", "fsdp"), None), P("rep", ("parts", "fsdp"), None))
    return jax.shard_map(local, mesh=mesh, in_specs=in_specs, out_specs=out_specs, check_vma=False)
```

time: 98.9 us -> 19.5 us (0.20)
  waiting for transfers between devices: 70.7 us -> 6.81 us
  between operations: 14.1 us -> 0.77 us
  starting transfers between devices: 0.04 us -> 7.53 us
  blocking collectives: 3.76 us -> 0 us
  matrix products: 4.54 us -> 1.47 us
  local copies, waits for them, and re-layouts: 2.65 us -> 1.02 us
  other arithmetic: 2.87 us -> 1.49 us
    unnamed x2 -> x0, waiting for transfers between devices: 70.7 us -> none
    ppermute x0 -> x7, starting transfers between devices: none -> 7.53 us  [send(): return lax.ppermute(x, ('fsdp', 'rep'), pairs)]
    ppermute x0 -> x7, waiting for transfers between devices: none -> 6.81 us  [send(): return lax.ppermute(x, ('fsdp', 'rep'), pairs)]
    all_gather x2 -> x0, blocking collectives: 3.76 us -> none  [the longest x1 1.95 us: local(): lax.all_gather(picks[None], 'rep', axis=0, tiled=True)]
    dot_general x7 -> x2, matrix products: 4.54 us -> 1.47 us  [the longest x1 1.02 us: near_rows(): lax.dot_general(picked, cot, (((1,), (1,)), ((), ())), preferred_element_...]
    add x1, other arithmetic: 1.6 us -> 0.04 us  [local(): part = part + x]
    unnamed x11 -> x16, local copies, waits for them, and re-layouts: 2.27 us -> 0.77 us
  transfers between devices with their start and end apart: 1 -> 7, of which waited for: 1 -> 5; matrix products, arithmetic and copies ran while one was open for 1% -> 5% of each run, Pallas kernels for 0% -> 0%
where the time goes in v1:
time: 19.5 us; the launch traced here: 19.4 us
  starting transfers between devices  7.53 us (39%)
  waiting for transfers between devices  6.81 us (35%)
  other arithmetic  1.49 us (8%)
  matrix products  1.47 us (8%)
  local copies, waits for them, and re-layouts  1.02 us (5%)
  between operations  0.77 us (4%)
  Pallas kernels  0.28 us (1%)
    ppermute x7, starting transfers between devices, send(): return lax.ppermute(x, ('fsdp', 'rep'), pairs)  7.53 us
    ppermute x7, waiting for transfers between devices, send(): return lax.ppermute(x, ('fsdp', 'rep'), pairs)  6.81 us
    dot_general x1, matrix products, near_rows(): lax.dot_general(picked, cot, (((1,), (1,)), ((), ())), preferred_element_...  1.02 us
    unnamed x16, local copies, waits for them, and re-layouts  0.77 us
    sub x1, other arithmetic, local(): params - learn_rate / reps * total  0.64 us
    sub x1, other arithmetic, local(): moved - lost  0.61 us
    dot_general x1, matrix products, near_rows(): lax.dot_general(left, tok, (((2,), (0,)), ((), ())), preferred_element_ty...  0.45 us
  transfers between devices with their start and end apart: 7, of which 5 were waited for; matrix products, arithmetic and copies ran while one was open for 5% of the time, Pallas kernels for 0%

profile of v1, /device:TPU:0, one launch (start us, length us, event | category | flops | bytes accessed | tf_op | source)
XLA Modules:
  0.0 19.4 jit_solution(8629155512943258622)
XLA Ops:
  0.6 0.0 copy-start
  0.6 0.0 copy-start.1
  0.7 0.0 copy-start.2
  0.7 0.0 copy-start.5
  0.7 0.0 copy-start.3
  0.7 0.0 copy-start.4
  0.7 1.0 %convolution_convert_fusion = bf16[8,256]{1,0:T(8,128)(2,1)S(1)} fusion(bf16[1,256,8]{1,2,0:T(8,128)(2,1)} %param.8, s32[8]{0:T(128)S(1)} %fusion.8), kind=kOutput, calls=%fused_computation.2 | convolution fusion | flops 34880 | bytes 8224 | tf_op jit(solution)/shard_map/dot_general | solution.py:79
  1.8 0.7 %copy-done = bf16[1,256,5120]{2,1,0:T(8,128)(2,1)S(1)} copy-done((bf16[1,256,5120]{2,1,0:T(8,128)(2,1)S(1)}, bf16[1,256,5120]{2,1,0:T(8,128)(2,1)}, u32[]{:S(2)}) %copy-start) | copy-done | bytes 2621464
  2.4 0.5 %fusion = f32[4,2,5120]{2,0,1:T(4,128)S(1)} fusion(bf16[1,256,5120]{2,1,0:T(8,128)(2,1)S(1)} %copy-done, bf16[4,2,256]{2,1,0:T(2,128)(2,1)S(1)} %reshape.47), kind=kOutput, calls=%fused_computation | convolution fusion | flops 20971520 | bytes 2789376 | tf_op jit(solution)/shard_map/dot_general | solution.py:81
  2.9 0.1 fusion.9
  3.0 0.6 %collective-permute-start = (f32[2,5120]{1,0:T(2,128)S(1)}, f32[2,5120]{1,0:T(2,128)S(1)}, u32[]{:S(2)}, u32[]{:S(2)}) collective-permute-start(f32[2,5120]{1,0:T(2,128)S(1)} %bitcast.30), channel_id=1, source_target_pairs={{0,1},{1,0},{2,3},{3,2},{4,5},{5,4},{6,7},{7,6},{8,9},{9,8},{10,11... | collective-permute-start | bytes 122888 | tf_op jit(solution)/shard_map/ppermute | solution.py:72
  3.6 2.7 %collective-permute-start.1 = (f32[2,5120]{1,0:T(2,128)S(1)}, f32[2,5120]{1,0:T(2,128)S(1)}, u32[]{:S(2)}, u32[]{:S(2)}) collective-permute-start(f32[2,5120]{1,0:T(2,128)S(1)} %bitcast.31), channel_id=1, source_target_pairs={{0,3},{1,2},{2,1},{3,0},{4,7},{5,6},{6,5},{7,4},{8,11},{9,10},{10,... | collective-permute-start | bytes 122888 | tf_op jit(solution)/shard_map/ppermute | solution.py:72
  6.3 1.3 %collective-permute-start.2 = (f32[2,5120]{1,0:T(2,128)S(1)}, f32[2,5120]{1,0:T(2,128)S(1)}, u32[]{:S(2)}, u32[]{:S(2)}) collective-permute-start(f32[2,5120]{1,0:T(2,128)S(1)} %bitcast.32), channel_id=1, source_target_pairs={{0,5},{1,4},{2,7},{3,6},{4,1},{5,0},{6,3},{7,2},{8,13},{9,12},{10,... | collective-permute-start | bytes 122888 | tf_op jit(solution)/shard_map/ppermute | solution.py:72
  7.6 0.1 collective-permute-start.3
  7.6 0.0 copy-done.5
  7.7 0.1 copy.18
  7.7 0.0 collective-permute-done
  7.7 0.4 %collective-permute-done.1 = f32[2,5120]{1,0:T(2,128)S(1)} collective-permute-done((f32[2,5120]{1,0:T(2,128)S(1)}, f32[2,5120]{1,0:T(2,128)S(1)}, u32[]{:S(2)}, u32[]{:S(2)}) %collective-permute-start.1) | collective-permute-done | bytes 40992 | tf_op jit(solution)/shard_map/ppermute | solution.py:72
  8.2 1.8 %collective-permute-done.2 = f32[2,5120]{1,0:T(2,128)S(1)} collective-permute-done((f32[2,5120]{1,0:T(2,128)S(1)}, f32[2,5120]{1,0:T(2,128)S(1)}, u32[]{:S(2)}, u32[]{:S(2)}) %collective-permute-start.2) | collective-permute-done | bytes 40992 | tf_op jit(solution)/shard_map/ppermute | solution.py:72
  10.0 2.0 %collective-permute-done.3 = f32[2,5120]{1,0:T(2,128)S(1)} collective-permute-done((f32[2,5120]{1,0:T(2,128)S(1)}, f32[2,5120]{1,0:T(2,128)S(1)}, u32[]{:S(2)}, u32[]{:S(2)}) %collective-permute-start.3) | collective-permute-done | bytes 40992 | tf_op jit(solution)/shard_map/ppermute | solution.py:72
  12.0 0.6 %collective-permute-start.4 = (f32[1,5120]{1,0:T(1,128)S(1)}, f32[1,5120]{1,0:T(1,128)S(1)}, u32[]{:S(2)}, u32[]{:S(2)}) collective-permute-start(f32[1,5120]{1,0:T(1,128)S(1)} %get-tuple-element.11), channel_id=1, source_target_pairs={{0,1},{1,0},{2,3},{3,2},{4,5},{5,4},{6,7},{7,6},{8,9},{9,8},{10,11... | collective-permute-start | bytes 61448 | tf_op jit(solution)/shard_map/ppermute | solution.py:72
  12.6 2.3 %collective-permute-start.5 = (f32[1,5120]{1,0:T(1,128)S(1)}, f32[1,5120]{1,0:T(1,128)S(1)}, u32[]{:S(2)}, u32[]{:S(2)}) collective-permute-start(f32[1,5120]{1,0:T(1,128)S(1)} %get-tuple-element.10), channel_id=1, source_target_pairs={{0,9},{1,8},{2,11},{3,10},{4,13},{5,12},{6,15},{7,14},{8,1},{9,0},... | collective-permute-start | bytes 61448 | tf_op jit(solution)/shard_map/ppermute | solution.py:72
  14.9 0.2 fusion.2
  15.1 0.0 collective-permute-done.4
  15.1 2.1 %collective-permute-done.5 = f32[1,5120]{1,0:T(1,128)S(1)} collective-permute-done((f32[1,5120]{1,0:T(1,128)S(1)}, f32[1,5120]{1,0:T(1,128)S(1)}, u32[]{:S(2)}, u32[]{:S(2)}) %collective-permute-start.5) | collective-permute-done | bytes 20512 | tf_op jit(solution)/shard_map/ppermute | solution.py:72
  17.2 0.0 copy-done.1
  17.2 0.0 copy-done.2
  17.2 0.0 copy-done.3
  17.2 0.3 %select.11 = (f32[40,128]{1,0:T(8,128)S(1)}, f32[40,128]{1,0:T(8,128)S(1)}) custom-call(f32[40,128]{1,0:T(8,128)S(1)} %bitcast.28, f32[40,128]{1,0:T(8,128)S(1)} %bitcast.29, f32[40,128]{1,0:T(8,128)S(1)} %bitcast.27, f32[40,128]{1,0:T(8,128)S(1)} %convert_element_type.8.refs_3_, bf16[256,256]{1,0:T(8,128)(2,1)S(1)} %copy-done.1, bf16[256,256]{1,0:T(8,128)(2,1)S(1)} %copy-done.2), custom_call_target="tpu_custom_call" | custom-call | tf_op jit(solution)/shard_map/select/pallas_call | solution.py:55
  17.5 0.2 collective-permute-start.6
  17.6 0.6 %sub.12 = f32[40,128]{1,0:T(8,128)} subtract(f32[40,128]{1,0:T(8,128)S(1)} %get-tuple-element.5, f32[40,128]{1,0:T(8,128)S(1)} %get-tuple-element.4) | non-fusion elementwise | flops 5120 | bytes 61440 | tf_op jit(solution)/shard_map/sub | solution.py:105
  18.3 0.5 %collective-permute-done.6 = f32[1,5120]{1,0:T(1,128)S(1)} collective-permute-done((f32[1,5120]{1,0:T(1,128)S(1)}, f32[1,5120]{1,0:T(1,128)S(1)}, u32[]{:S(2)}, u32[]{:S(2)}) %collective-permute-start.6) | collective-permute-done | bytes 20512 | tf_op jit(solution)/shard_map/ppermute | solution.py:72
  18.7 0.0 copy-done.4
  18.7 0.6 %multiply_subtract_fusion = f32[1,5120]{1,0:T(1,128)} fusion(f32[1,5120]{1,0:T(1,128)S(1)} %copy-done.4, f32[1,5120]{1,0:T(1,128)S(1)} %bitcast.26, f32[1,5120]{1,0:T(1,128)S(1)} %collective-permute-done.6), kind=kLoop, calls=%fused_computation.10 | loop fusion | flops 15360 | bytes 81920 | tf_op jit(solution)/shard_map/sub | solution.py:105
  (9 shorter events, 0.2 us)
Async XLA Ops:
  0.6 1.8 %copy-start = (bf16[1,256,5120]{2,1,0:T(8,128)(2,1)S(1)}, bf16[1,256,5120]{2,1,0:T(8,128)(2,1)}, u32[]{:S(2)}) copy-start(bf16[1,256,5120]{2,1,0:T(8,128)(2,1)} %param.7) | copy-start | bytes 7864324
  0.6 16.6 %copy-start.1 = (bf16[256,256]{1,0:T(8,128)(2,1)S(1)}, bf16[256,256]{1,0:T(8,128)(2,1)}, u32[]{:S(2)}) copy-start(bf16[256,256]{1,0:T(8,128)(2,1)} %constant.45.clone.refs_4_) | copy-start | bytes 393220
  0.7 16.5 %copy-start.2 = (bf16[256,256]{1,0:T(8,128)(2,1)S(1)}, bf16[256,256]{1,0:T(8,128)(2,1)}, u32[]{:S(2)}) copy-start(bf16[256,256]{1,0:T(8,128)(2,1)} %constant.46.clone.refs_5_) | copy-start | bytes 393220
  0.7 7.0 %copy-start.5 = (s32[1,1,40,16]{2,3,1,0:T(8,128)S(1)}, s32[1,1,40,16]{2,3,1,0:T(8,128)}, u32[]{:S(2)}) copy-start(s32[1,1,40,16]{2,3,1,0:T(8,128)} %param.11) | copy-start | bytes 7684
  0.7 16.5 %copy-start.3 = (f32[1,1,5120]{2,1,0:T(1,128)S(1)}, f32[1,1,5120]{2,1,0:T(1,128)}, u32[]{:S(2)}) copy-start(f32[1,1,5120]{2,1,0:T(1,128)} %param.10) | copy-start | bytes 61444
  0.7 18.0 %copy-start.4 = (f32[1,5120]{1,0:T(1,128)S(1)}, f32[1,5120]{1,0:T(1,128)}, u32[]{:S(2)}) copy-start(f32[1,5120]{1,0:T(1,128)} %param.9) | copy-start | bytes 61444
  3.0 4.7 %collective-permute-start = (f32[2,5120]{1,0:T(2,128)S(1)}, f32[2,5120]{1,0:T(2,128)S(1)}, u32[]{:S(2)}, u32[]{:S(2)}) collective-permute-start(f32[2,5120]{1,0:T(2,128)S(1)} %bitcast.30), channel_id=1, source_target_pairs={{0,1},{1,0},{2,3},{3,2},{4,5},{5,4},{6,7},{7,6},{8,9},{9,8},{10,11... | collective-permute-start | bytes 122888 | tf_op jit(solution)/shard_map/ppermute | solution.py:72
  3.6 4.6 %collective-permute-start.1 = (f32[2,5120]{1,0:T(2,128)S(1)}, f32[2,5120]{1,0:T(2,128)S(1)}, u32[]{:S(2)}, u32[]{:S(2)}) collective-permute-start(f32[2,5120]{1,0:T(2,128)S(1)} %bitcast.31), channel_id=1, source_target_pairs={{0,3},{1,2},{2,1},{3,0},{4,7},{5,6},{6,5},{7,4},{8,11},{9,10},{10,... | collective-permute-start | bytes 122888 | tf_op jit(solution)/shard_map/ppermute | solution.py:72
  6.3 3.7 %collective-permute-start.2 = (f32[2,5120]{1,0:T(2,128)S(1)}, f32[2,5120]{1,0:T(2,128)S(1)}, u32[]{:S(2)}, u32[]{:S(2)}) collective-permute-start(f32[2,5120]{1,0:T(2,128)S(1)} %bitcast.32), channel_id=1, source_target_pairs={{0,5},{1,4},{2,7},{3,6},{4,1},{5,0},{6,3},{7,2},{8,13},{9,12},{10,... | collective-permute-start | bytes 122888 | tf_op jit(solution)/shard_map/ppermute | solution.py:72
  7.6 4.4 %collective-permute-start.3 = (f32[2,5120]{1,0:T(2,128)S(1)}, f32[2,5120]{1,0:T(2,128)S(1)}, u32[]{:S(2)}, u32[]{:S(2)}) collective-permute-start(f32[2,5120]{1,0:T(2,128)S(1)} %bitcast.33), channel_id=1, source_target_pairs={{0,7},{1,6},{2,5},{3,4},{4,3},{5,2},{6,1},{7,0},{8,15},{9,14},{10,... | collective-permute-start | bytes 122888 | tf_op jit(solution)/shard_map/ppermute | solution.py:72
  12.0 3.0 %collective-permute-start.4 = (f32[1,5120]{1,0:T(1,128)S(1)}, f32[1,5120]{1,0:T(1,128)S(1)}, u32[]{:S(2)}, u32[]{:S(2)}) collective-permute-start(f32[1,5120]{1,0:T(1,128)S(1)} %get-tuple-element.11), channel_id=1, source_target_pairs={{0,1},{1,0},{2,3},{3,2},{4,5},{5,4},{6,7},{7,6},{8,9},{9,8},{10,11... | collective-permute-start | bytes 61448 | tf_op jit(solution)/shard_map/ppermute | solution.py:72
  12.6 4.6 %collective-permute-start.5 = (f32[1,5120]{1,0:T(1,128)S(1)}, f32[1,5120]{1,0:T(1,128)S(1)}, u32[]{:S(2)}, u32[]{:S(2)}) collective-permute-start(f32[1,5120]{1,0:T(1,128)S(1)} %get-tuple-element.10), channel_id=1, source_target_pairs={{0,9},{1,8},{2,11},{3,10},{4,13},{5,12},{6,15},{7,14},{8,1},{9,0},... | collective-permute-start | bytes 61448 | tf_op jit(solution)/shard_map/ppermute | solution.py:72
  17.5 1.2 %collective-permute-start.6 = (f32[1,5120]{1,0:T(1,128)S(1)}, f32[1,5120]{1,0:T(1,128)S(1)}, u32[]{:S(2)}, u32[]{:S(2)}) collective-permute-start(f32[1,5120]{1,0:T(1,128)S(1)} %bitcast.25), channel_id=1, source_target_pairs={{0,1},{1,0},{2,3},{3,2},{4,5},{5,4},{6,7},{7,6},{8,9},{9,8},{10,11... | collective-permute-start | bytes 61448 | tf_op jit(solution)/shard_map/ppermute | solution.py:72

commit v2 on v1

--- a/solution.py
+++ b/solution.py
@@ -22,15 +22,15 @@
 def split_factor(matrix):
     high = matrix.astype(jnp.bfloat16)
     low = (matrix - high.astype(np.float64)).astype(jnp.bfloat16)
-    return np.block([[high, low], [high, low]])
+    return np.concatenate([high, low], 1)
 
 
 def split_dot(x, factor):
     high = x.astype(jnp.bfloat16)
     low = (x - high.astype(jnp.float32)).astype(jnp.bfloat16)
-    y = jnp.dot(jnp.concatenate([high, low], 1), factor, preferred_element_type=jnp.float32)
-    half = y.shape[1] // 2
-    return y[:, :half] + y[:, half:]
+    y = jnp.dot(jnp.concatenate([high, low], 0), factor, preferred_element_type=jnp.float32)
+    rows, half = x.shape[0], y.shape[1] // 2
+    return (y[:rows, :half] + y[rows:, :half]) + (y[:rows, half:] + y[rows:, half:])
 
 
 def select_kernel(count, *refs):
@@ -72,13 +72,55 @@
     return lax.ppermute(x, ("fsdp", "rep"), pairs)
 
 
+def chunk_starts(width):
+    blocks = width // SPAN
+    return [blocks * f // 40 * SPAN for f in (0, 6, 16, 28, 40)]
+
+
+def rows_kernel(n, where, cot_hbm, tok, *refs):
+    outs, (cot, held, sems) = refs[:-3], refs[-3:]
+    width = held.shape[1]
+    starts = chunk_starts(width)
+    first = pltpu.make_async_copy(cot_hbm, cot, sems.at[len(starts) - 1])
+    first.start()
+    copies = []
+    for c, (a, b) in enumerate(zip(starts, starts[1:])):
+        cols = pl.ds(a, b - a)
+        copies.append(pltpu.make_async_copy(tok.at[:, cols], held.at[:, cols], sems.at[c]))
+        copies[-1].start()
+    row = lax.broadcasted_iota(jnp.int32, (n, n), 0)
+    col = lax.broadcasted_iota(jnp.int32, (n, n), 1)
+    high = n // 4
+    picked = ((row // high) ^ (row % high * 4) ^ where[0]) == col
+    first.wait()
+    left = jnp.dot(picked.astype(cot.dtype), cot[...], preferred_element_type=jnp.float32).astype(cot.dtype)
+    for copy, a, b in zip(copies, starts, starts[1:]):
+        copy.wait()
+        cols = pl.ds(a, b - a)
+        y = jnp.dot(left, held[:, cols], preferred_element_type=jnp.float32)
+        for k, out in enumerate(outs):
+            out[:, cols] = y[high * k : high * (k + 1)]
+
+
 def near_rows(cot, tok, me, n):
-    place = jnp.arange(n, dtype=jnp.int32)
-    wanted = (place // (n // 4)) ^ (place % (n // 4) * 4) ^ me
-    picked = (wanted[:, None] == place).astype(cot.dtype)
-    left = lax.dot_general(picked, cot, (((1,), (1,)), ((), ())), preferred_element_type=jnp.float32)
-    left = lax.optimization_barrier(left.astype(cot.dtype).reshape(4, n // 4, -1))
-    return lax.dot_general(left, tok, (((2,), (0,)), ((), ())), preferred_element_type=jnp.float32)
+    depth, width = tok.shape
+    vmem = pl.BlockSpec(memory_space=pltpu.VMEM)
+    hbm = pl.BlockSpec(memory_space=pltpu.HBM)
+    tok = pltpu.with_memory_space_constraint(tok, pltpu.HBM)
+    cot = pltpu.with_memory_space_constraint(cot.T, pltpu.HBM)
+    return pl.pallas_call(
+        lambda *refs: rows_kernel(n, *refs),
+        out_shape=[jax.ShapeDtypeStruct((n // 4, width), jnp.float32)] * 4,
+        in_specs=[pl.BlockSpec(memory_space=pltpu.SMEM), hbm, hbm],
+        out_specs=[vmem] * 4,
+        scratch_shapes=[
+            pltpu.VMEM((n, depth), tok.dtype),
+            pltpu.VMEM((depth, width), tok.dtype),
+            pltpu.SemaphoreType.DMA((len(chunk_starts(width)),)),
+        ],
+        compiler_params=pltpu.CompilerParams(vmem_limit_bytes=8 << 20),
+        name="near_rows",
+    )(me.reshape(1), cot, tok)
 
 
 def local(tokens, cotangent, params, momentum, indices):

time: 19.5 us -> 19 us (0.974)
  Pallas kernels: 0.28 us -> 2.3 us
  matrix products: 1.47 us -> 0 us
  local copies, waits for them, and re-layouts: 1.02 us -> 0.14 us
    pallas_call x0 -> x1, Pallas kernels: none -> 2.02 us  [near_rows(): pl.pallas_call(lambda *refs: rows_kernel(n, *refs), out_shape=[jax.ShapeD...]
    dot_general x2 -> x0, matrix products: 1.47 us -> none  [the longest x1 1.02 us: near_rows(): lax.dot_general(picked, cot, (((1,), (1,)), ((), ())), preferred_element_...]
    unnamed x16 -> x10, local copies, waits for them, and re-layouts: 0.77 us -> 0.03 us
where the time goes in v2:
time: 19 us; the launch traced here: 18.8 us
  starting transfers between devices  7.36 us (39%)
  waiting for transfers between devices  6.83 us (36%)
  Pallas kernels  2.3 us (12%)
  other arithmetic  1.48 us (8%)
  between operations  0.73 us (4%)
    ppermute x7, starting transfers between devices, send(): return lax.ppermute(x, ('fsdp', 'rep'), pairs)  7.36 us
    ppermute x7, waiting for transfers between devices, send(): return lax.ppermute(x, ('fsdp', 'rep'), pairs)  6.83 us
    pallas_call x1, Pallas kernels, near_rows(): pl.pallas_call(lambda *refs: rows_kernel(n, *refs), out_shape=[jax.ShapeD...  2.02 us
    sub x1, other arithmetic, local(): params - learn_rate / reps * total  0.64 us
    sub x1, other arithmetic, local(): moved - lost  0.61 us
  transfers between devices with their start and end apart: 7, of which 5 were waited for; matrix products, arithmetic and copies ran while one was open for 5% of the time, Pallas kernels for 0%

profile of v2, /device:TPU:0, one launch (start us, length us, event | category | flops | bytes accessed | tf_op | source)
XLA Modules:
  0.0 18.8 jit_solution(1712948749800271806)
XLA Ops:
  0.6 0.0 copy-start
  0.6 0.0 copy-start.1
  0.7 0.0 copy-start.4
  0.7 0.0 copy-start.2
  0.7 0.0 copy-start.3
  0.7 2.0 %near_rows.1 = (f32[2,5120]{1,0:T(2,128)S(1)}, f32[2,5120]{1,0:T(2,128)S(1)}, f32[2,5120]{1,0:T(2,128)S(1)}, f32[2,5120]{1,0:T(2,128)S(1)}) custom-call(s32[1]{0:T(128)} %bitcast.refs_0_, bf16[8,256]{1,0:T(8,128)(2,1)} %bitcast.19, bf16[256,5120]{1,0:T(8,128)(2,1)} %bitcast.16), custom_call_target="tpu_custom_call" | custom-call | tf_op jit(solution)/shard_map/near_rows/pallas_call | solution.py:111
  2.7 0.6 %collective-permute-start = (f32[2,5120]{1,0:T(2,128)S(1)}, f32[2,5120]{1,0:T(2,128)S(1)}, u32[]{:S(2)}, u32[]{:S(2)}) collective-permute-start(f32[2,5120]{1,0:T(2,128)S(1)} %get-tuple-element.8), channel_id=1, source_target_pairs={{0,1},{1,0},{2,3},{3,2},{4,5},{5,4},{6,7},{7,6},{8,9},{9,8},{10,11... | collective-permute-start | bytes 122888 | tf_op jit(solution)/shard_map/ppermute | solution.py:72
  3.3 2.6 %collective-permute-start.1 = (f32[2,5120]{1,0:T(2,128)S(1)}, f32[2,5120]{1,0:T(2,128)S(1)}, u32[]{:S(2)}, u32[]{:S(2)}) collective-permute-start(f32[2,5120]{1,0:T(2,128)S(1)} %get-tuple-element.9), channel_id=1, source_target_pairs={{0,3},{1,2},{2,1},{3,0},{4,7},{5,6},{6,5},{7,4},{8,11},{9,10},{10,... | collective-permute-start | bytes 122888 | tf_op jit(solution)/shard_map/ppermute | solution.py:72
  5.9 1.3 %collective-permute-start.2 = (f32[2,5120]{1,0:T(2,128)S(1)}, f32[2,5120]{1,0:T(2,128)S(1)}, u32[]{:S(2)}, u32[]{:S(2)}) collective-permute-start(f32[2,5120]{1,0:T(2,128)S(1)} %get-tuple-element.10), channel_id=1, source_target_pairs={{0,5},{1,4},{2,7},{3,6},{4,1},{5,0},{6,3},{7,2},{8,13},{9,12},{10,... | collective-permute-start | bytes 122888 | tf_op jit(solution)/shard_map/ppermute | solution.py:72
  7.1 0.0 collective-permute-start.3
  7.1 0.0 copy-done.4
  7.1 0.1 copy.10
  7.2 0.0 collective-permute-done
  7.2 0.5 %collective-permute-done.1 = f32[2,5120]{1,0:T(2,128)S(1)} collective-permute-done((f32[2,5120]{1,0:T(2,128)S(1)}, f32[2,5120]{1,0:T(2,128)S(1)}, u32[]{:S(2)}, u32[]{:S(2)}) %collective-permute-start.1) | collective-permute-done | bytes 40992 | tf_op jit(solution)/shard_map/ppermute | solution.py:72
  7.7 1.7 %collective-permute-done.2 = f32[2,5120]{1,0:T(2,128)S(1)} collective-permute-done((f32[2,5120]{1,0:T(2,128)S(1)}, f32[2,5120]{1,0:T(2,128)S(1)}, u32[]{:S(2)}, u32[]{:S(2)}) %collective-permute-start.2) | collective-permute-done | bytes 40992 | tf_op jit(solution)/shard_map/ppermute | solution.py:72
  9.5 2.0 %collective-permute-done.3 = f32[2,5120]{1,0:T(2,128)S(1)} collective-permute-done((f32[2,5120]{1,0:T(2,128)S(1)}, f32[2,5120]{1,0:T(2,128)S(1)}, u32[]{:S(2)}, u32[]{:S(2)}) %collective-permute-start.3) | collective-permute-done | bytes 40992 | tf_op jit(solution)/shard_map/ppermute | solution.py:72
  11.5 0.5 %collective-permute-start.4 = (f32[1,5120]{1,0:T(1,128)S(1)}, f32[1,5120]{1,0:T(1,128)S(1)}, u32[]{:S(2)}, u32[]{:S(2)}) collective-permute-start(f32[1,5120]{1,0:T(1,128)S(1)} %get-tuple-element.15), channel_id=1, source_target_pairs={{0,1},{1,0},{2,3},{3,2},{4,5},{5,4},{6,7},{7,6},{8,9},{9,8},{10,11... | collective-permute-start | bytes 61448 | tf_op jit(solution)/shard_map/ppermute | solution.py:72
  12.0 2.3 %collective-permute-start.5 = (f32[1,5120]{1,0:T(1,128)S(1)}, f32[1,5120]{1,0:T(1,128)S(1)}, u32[]{:S(2)}, u32[]{:S(2)}) collective-permute-start(f32[1,5120]{1,0:T(1,128)S(1)} %get-tuple-element.14), channel_id=1, source_target_pairs={{0,9},{1,8},{2,11},{3,10},{4,13},{5,12},{6,15},{7,14},{8,1},{9,0},... | collective-permute-start | bytes 61448 | tf_op jit(solution)/shard_map/ppermute | solution.py:72
  14.3 0.2 fusion
  14.5 0.0 collective-permute-done.4
  14.5 2.1 %collective-permute-done.5 = f32[1,5120]{1,0:T(1,128)S(1)} collective-permute-done((f32[1,5120]{1,0:T(1,128)S(1)}, f32[1,5120]{1,0:T(1,128)S(1)}, u32[]{:S(2)}, u32[]{:S(2)}) %collective-permute-start.5) | collective-permute-done | bytes 20512 | tf_op jit(solution)/shard_map/ppermute | solution.py:72
  16.6 0.0 copy-done
  16.6 0.0 copy-done.1
  16.6 0.0 copy-done.2
  16.6 0.3 %select.1 = (f32[40,128]{1,0:T(8,128)S(1)}, f32[40,128]{1,0:T(8,128)S(1)}) custom-call(f32[40,128]{1,0:T(8,128)S(1)} %bitcast.14, f32[40,128]{1,0:T(8,128)S(1)} %bitcast.15, f32[40,128]{1,0:T(8,128)S(1)} %bitcast.13, f32[40,128]{1,0:T(8,128)S(1)} %convert_element_type.3.refs_3_, bf16[128,256]{1,0:T(8,128)(2,1)S(1)} %copy-done, bf16[128,256]{1,0:T(8,128)(2,1)S(1)} %copy-done.1), custom_call_target="tpu_custom_call" | custom-call | tf_op jit(solution)/shard_map/select/pallas_call | solution.py:55
  16.9 0.2 collective-permute-start.6
  17.1 0.6 %sub.7 = f32[40,128]{1,0:T(8,128)} subtract(f32[40,128]{1,0:T(8,128)S(1)} %get-tuple-element.13, f32[40,128]{1,0:T(8,128)S(1)} %get-tuple-element.12) | non-fusion elementwise | flops 5120 | bytes 61440 | tf_op jit(solution)/shard_map/sub | solution.py:147
  17.7 0.5 %collective-permute-done.6 = f32[1,5120]{1,0:T(1,128)S(1)} collective-permute-done((f32[1,5120]{1,0:T(1,128)S(1)}, f32[1,5120]{1,0:T(1,128)S(1)}, u32[]{:S(2)}, u32[]{:S(2)}) %collective-permute-start.6) | collective-permute-done | bytes 20512 | tf_op jit(solution)/shard_map/ppermute | solution.py:72
  18.2 0.0 copy-done.3
  18.2 0.6 %multiply_subtract_fusion = f32[1,5120]{1,0:T(1,128)} fusion(f32[1,5120]{1,0:T(1,128)S(1)} %copy-done.3, f32[1,5120]{1,0:T(1,128)S(1)} %bitcast.12, f32[1,5120]{1,0:T(1,128)S(1)} %collective-permute-done.6), kind=kLoop, calls=%fused_computation.3 | loop fusion | flops 15360 | bytes 81920 | tf_op jit(solution)/shard_map/sub | solution.py:147
  (3 shorter events, 0.1 us)
Async XLA Ops:
  0.6 16.0 %copy-start = (bf16[128,256]{1,0:T(8,128)(2,1)S(1)}, bf16[128,256]{1,0:T(8,128)(2,1)}, u32[]{:S(2)}) copy-start(bf16[128,256]{1,0:T(8,128)(2,1)} %constant.14.clone.refs_4_) | copy-start | bytes 196612
  0.6 16.0 %copy-start.1 = (bf16[128,256]{1,0:T(8,128)(2,1)S(1)}, bf16[128,256]{1,0:T(8,128)(2,1)}, u32[]{:S(2)}) copy-start(bf16[128,256]{1,0:T(8,128)(2,1)} %constant.15.clone.refs_5_) | copy-start | bytes 196612
  0.7 6.5 %copy-start.4 = (s32[1,1,40,16]{2,3,1,0:T(8,128)S(1)}, s32[1,1,40,16]{2,3,1,0:T(8,128)}, u32[]{:S(2)}) copy-start(s32[1,1,40,16]{2,3,1,0:T(8,128)} %param.11) | copy-start | bytes 7684
  0.7 16.0 %copy-start.2 = (f32[1,1,5120]{2,1,0:T(1,128)S(1)}, f32[1,1,5120]{2,1,0:T(1,128)}, u32[]{:S(2)}) copy-start(f32[1,1,5120]{2,1,0:T(1,128)} %param.10) | copy-start | bytes 61444
  0.7 17.5 %copy-start.3 = (f32[1,5120]{1,0:T(1,128)S(1)}, f32[1,5120]{1,0:T(1,128)}, u32[]{:S(2)}) copy-start(f32[1,5120]{1,0:T(1,128)} %param.9) | copy-start | bytes 61444
  2.7 4.5 %collective-permute-start = (f32[2,5120]{1,0:T(2,128)S(1)}, f32[2,5120]{1,0:T(2,128)S(1)}, u32[]{:S(2)}, u32[]{:S(2)}) collective-permute-start(f32[2,5120]{1,0:T(2,128)S(1)} %get-tuple-element.8), channel_id=1, source_target_pairs={{0,1},{1,0},{2,3},{3,2},{4,5},{5,4},{6,7},{7,6},{8,9},{9,8},{10,11... | collective-permute-start | bytes 122888 | tf_op jit(solution)/shard_map/ppermute | solution.py:72
  3.3 4.4 %collective-permute-start.1 = (f32[2,5120]{1,0:T(2,128)S(1)}, f32[2,5120]{1,0:T(2,128)S(1)}, u32[]{:S(2)}, u32[]{:S(2)}) collective-permute-start(f32[2,5120]{1,0:T(2,128)S(1)} %get-tuple-element.9), channel_id=1, source_target_pairs={{0,3},{1,2},{2,1},{3,0},{4,7},{5,6},{6,5},{7,4},{8,11},{9,10},{10,... | collective-permute-start | bytes 122888 | tf_op jit(solution)/shard_map/ppermute | solution.py:72
  5.9 3.6 %collective-permute-start.2 = (f32[2,5120]{1,0:T(2,128)S(1)}, f32[2,5120]{1,0:T(2,128)S(1)}, u32[]{:S(2)}, u32[]{:S(2)}) collective-permute-start(f32[2,5120]{1,0:T(2,128)S(1)} %get-tuple-element.10), channel_id=1, source_target_pairs={{0,5},{1,4},{2,7},{3,6},{4,1},{5,0},{6,3},{7,2},{8,13},{9,12},{10,... | collective-permute-start | bytes 122888 | tf_op jit(solution)/shard_map/ppermute | solution.py:72
  7.1 4.3 %collective-permute-start.3 = (f32[2,5120]{1,0:T(2,128)S(1)}, f32[2,5120]{1,0:T(2,128)S(1)}, u32[]{:S(2)}, u32[]{:S(2)}) collective-permute-start(f32[2,5120]{1,0:T(2,128)S(1)} %get-tuple-element.11), channel_id=1, source_target_pairs={{0,7},{1,6},{2,5},{3,4},{4,3},{5,2},{6,1},{7,0},{8,15},{9,14},{10,... | collective-permute-start | bytes 122888 | tf_op jit(solution)/shard_map/ppermute | solution.py:72
  11.5 3.0 %collective-permute-start.4 = (f32[1,5120]{1,0:T(1,128)S(1)}, f32[1,5120]{1,0:T(1,128)S(1)}, u32[]{:S(2)}, u32[]{:S(2)}) collective-permute-start(f32[1,5120]{1,0:T(1,128)S(1)} %get-tuple-element.15), channel_id=1, source_target_pairs={{0,1},{1,0},{2,3},{3,2},{4,5},{5,4},{6,7},{7,6},{8,9},{9,8},{10,11... | collective-permute-start | bytes 61448 | tf_op jit(solution)/shard_map/ppermute | solution.py:72
  12.0 4.6 %collective-permute-start.5 = (f32[1,5120]{1,0:T(1,128)S(1)}, f32[1,5120]{1,0:T(1,128)S(1)}, u32[]{:S(2)}, u32[]{:S(2)}) collective-permute-start(f32[1,5120]{1,0:T(1,128)S(1)} %get-tuple-element.14), channel_id=1, source_target_pairs={{0,9},{1,8},{2,11},{3,10},{4,13},{5,12},{6,15},{7,14},{8,1},{9,0},... | collective-permute-start | bytes 61448 | tf_op jit(solution)/shard_map/ppermute | solution.py:72
  16.9 1.3 %collective-permute-start.6 = (f32[1,5120]{1,0:T(1,128)S(1)}, f32[1,5120]{1,0:T(1,128)S(1)}, u32[]{:S(2)}, u32[]{:S(2)}) collective-permute-start(f32[1,5120]{1,0:T(1,128)S(1)} %bitcast.11), channel_id=1, source_target_pairs={{0,1},{1,0},{2,3},{3,2},{4,5},{5,4},{6,7},{7,6},{8,9},{9,8},{10,11... | collective-permute-start | bytes 61448 | tf_op jit(solution)/shard_map/ppermute | solution.py:72

commit v3 on v2

--- a/solution.py
+++ b/solution.py
@@ -67,8 +67,13 @@
     return n in (4, 8, 16)
 
 
+def turned(i, k):
+    return 3 - k if k in (1, 2) and (i ^ (i >> 1)) & 1 else k
+
+
 def send(x, n, reps, offset):
-    pairs = [(i * reps + c, (i ^ offset) * reps + (c + 1) % reps) for i in range(n) for c in range(reps)]
+    to = [i ^ turned(i, offset) for i in range(n)]
+    pairs = [(i * reps + c, to[i] * reps + (c + 1) % reps) for i in range(n) for c in range(reps)]
     return lax.ppermute(x, ("fsdp", "rep"), pairs)
 
 
@@ -91,7 +96,11 @@
     row = lax.broadcasted_iota(jnp.int32, (n, n), 0)
     col = lax.broadcasted_iota(jnp.int32, (n, n), 1)
     high = n // 4
-    picked = ((row // high) ^ (row % high * 4) ^ where[0]) == col
+    piece, me = row // high, where[0]
+    swapped = jnp.where((piece == 1) | (piece == 2), 3 - piece, piece)
+    odd = (me ^ (me // 2)) % 2
+    piece = jnp.where(odd == 1, swapped, piece)
+    picked = (piece ^ (row % high * 4) ^ me) == col
     first.wait()
     left = jnp.dot(picked.astype(cot.dtype), cot[...], preferred_element_type=jnp.float32).astype(cot.dtype)
     for copy, a, b in zip(copies, starts, starts[1:]):

time: 19 us -> 18.4 us (0.968)
  waiting for transfers between devices: 6.83 us -> 4.22 us
  starting transfers between devices: 7.36 us -> 9.36 us
    ppermute x7, waiting for transfers between devices: 6.83 us -> 4.22 us  [send(): return lax.ppermute(x, ('fsdp', 'rep'), pairs)]
    ppermute x7, starting transfers between devices: 7.36 us -> 9.36 us  [send(): return lax.ppermute(x, ('fsdp', 'rep'), pairs)]
  transfers between devices with their start and end apart: 7 -> 7, of which waited for: 5 -> 4; matrix products, arithmetic and copies ran while one was open for 5% -> 5% of each run, Pallas kernels for 0% -> 0%
where the time goes in v3:
time: 18.4 us; the launch traced here: 18.2 us
  starting transfers between devices  9.36 us (51%)
  waiting for transfers between devices  4.22 us (23%)
  Pallas kernels  2.3 us (12%)
  other arithmetic  1.48 us (8%)
  between operations  0.73 us (4%)
    ppermute x7, starting transfers between devices, send(): return lax.ppermute(x, ('fsdp', 'rep'), pairs)  9.36 us
    ppermute x7, waiting for transfers between devices, send(): return lax.ppermute(x, ('fsdp', 'rep'), pairs)  4.22 us
    pallas_call x1, Pallas kernels, near_rows(): pl.pallas_call(lambda *refs: rows_kernel(n, *refs), out_shape=[jax.ShapeD...  2.02 us
    sub x1, other arithmetic, local(): params - learn_rate / reps * total  0.64 us
    sub x1, other arithmetic, local(): moved - lost  0.61 us
  transfers between devices with their start and end apart: 7, of which 4 were waited for; matrix products, arithmetic and copies ran while one was open for 5% of the time, Pallas kernels for 0%

profile of v3, /device:TPU:0, one launch (start us, length us, event | category | flops | bytes accessed | tf_op | source)
XLA Modules:
  0.0 18.2 jit_solution(16427243334559119800)
XLA Ops:
  0.6 0.0 copy-start
  0.6 0.0 copy-start.1
  0.7 0.0 copy-start.4
  0.7 0.0 copy-start.2
  0.7 0.0 copy-start.3
  0.7 2.0 %near_rows.1 = (f32[2,5120]{1,0:T(2,128)S(1)}, f32[2,5120]{1,0:T(2,128)S(1)}, f32[2,5120]{1,0:T(2,128)S(1)}, f32[2,5120]{1,0:T(2,128)S(1)}) custom-call(s32[1]{0:T(128)} %bitcast.refs_0_, bf16[8,256]{1,0:T(8,128)(2,1)} %bitcast.19, bf16[256,5120]{1,0:T(8,128)(2,1)} %bitcast.16), custom_call_target="tpu_custom_call" | custom-call | tf_op jit(solution)/shard_map/near_rows/pallas_call | solution.py:120
  2.7 0.6 %collective-permute-start = (f32[2,5120]{1,0:T(2,128)S(1)}, f32[2,5120]{1,0:T(2,128)S(1)}, u32[]{:S(2)}, u32[]{:S(2)}) collective-permute-start(f32[2,5120]{1,0:T(2,128)S(1)} %get-tuple-element.8), channel_id=1, source_target_pairs={{0,1},{1,0},{2,3},{3,2},{4,5},{5,4},{6,7},{7,6},{8,9},{9,8},{10,11... | collective-permute-start | bytes 122888 | tf_op jit(solution)/shard_map/ppermute | solution.py:77
  3.3 2.6 %collective-permute-start.1 = (f32[2,5120]{1,0:T(2,128)S(1)}, f32[2,5120]{1,0:T(2,128)S(1)}, u32[]{:S(2)}, u32[]{:S(2)}) collective-permute-start(f32[2,5120]{1,0:T(2,128)S(1)} %get-tuple-element.9), channel_id=1, source_target_pairs={{0,3},{1,2},{2,7},{3,6},{4,1},{5,0},{6,5},{7,4},{8,11},{9,10},{10,... | collective-permute-start | bytes 122888 | tf_op jit(solution)/shard_map/ppermute | solution.py:77
  5.9 0.1 collective-permute-start.2
  6.0 2.7 %collective-permute-start.3 = (f32[2,5120]{1,0:T(2,128)S(1)}, f32[2,5120]{1,0:T(2,128)S(1)}, u32[]{:S(2)}, u32[]{:S(2)}) collective-permute-start(f32[2,5120]{1,0:T(2,128)S(1)} %get-tuple-element.11), channel_id=1, source_target_pairs={{0,7},{1,6},{2,5},{3,4},{4,3},{5,2},{6,1},{7,0},{8,15},{9,14},{10,... | collective-permute-start | bytes 122888 | tf_op jit(solution)/shard_map/ppermute | solution.py:77
  8.6 0.0 copy-done.4
  8.6 0.1 copy.10
  8.7 0.0 collective-permute-done
  8.7 0.0 collective-permute-done.1
  8.7 0.8 %collective-permute-done.2 = f32[2,5120]{1,0:T(2,128)S(1)} collective-permute-done((f32[2,5120]{1,0:T(2,128)S(1)}, f32[2,5120]{1,0:T(2,128)S(1)}, u32[]{:S(2)}, u32[]{:S(2)}) %collective-permute-start.2) | collective-permute-done | bytes 40992 | tf_op jit(solution)/shard_map/ppermute | solution.py:77
  9.5 1.9 %collective-permute-done.3 = f32[2,5120]{1,0:T(2,128)S(1)} collective-permute-done((f32[2,5120]{1,0:T(2,128)S(1)}, f32[2,5120]{1,0:T(2,128)S(1)}, u32[]{:S(2)}, u32[]{:S(2)}) %collective-permute-start.3) | collective-permute-done | bytes 40992 | tf_op jit(solution)/shard_map/ppermute | solution.py:77
  11.5 0.2 collective-permute-start.4
  11.6 2.6 %collective-permute-start.5 = (f32[1,5120]{1,0:T(1,128)S(1)}, f32[1,5120]{1,0:T(1,128)S(1)}, u32[]{:S(2)}, u32[]{:S(2)}) collective-permute-start(f32[1,5120]{1,0:T(1,128)S(1)} %get-tuple-element.14), channel_id=1, source_target_pairs={{0,9},{1,8},{2,11},{3,10},{4,13},{5,12},{6,15},{7,14},{8,1},{9,0},... | collective-permute-start | bytes 61448 | tf_op jit(solution)/shard_map/ppermute | solution.py:77
  14.2 0.2 fusion
  14.4 0.0 collective-permute-done.4
  14.4 1.3 %collective-permute-done.5 = f32[1,5120]{1,0:T(1,128)S(1)} collective-permute-done((f32[1,5120]{1,0:T(1,128)S(1)}, f32[1,5120]{1,0:T(1,128)S(1)}, u32[]{:S(2)}, u32[]{:S(2)}) %collective-permute-start.5) | collective-permute-done | bytes 20512 | tf_op jit(solution)/shard_map/ppermute | solution.py:77
  15.7 0.0 copy-done
  15.8 0.0 copy-done.1
  15.8 0.0 copy-done.2
  15.8 0.3 %select.1 = (f32[40,128]{1,0:T(8,128)S(1)}, f32[40,128]{1,0:T(8,128)S(1)}) custom-call(f32[40,128]{1,0:T(8,128)S(1)} %bitcast.14, f32[40,128]{1,0:T(8,128)S(1)} %bitcast.15, f32[40,128]{1,0:T(8,128)S(1)} %bitcast.13, f32[40,128]{1,0:T(8,128)S(1)} %convert_element_type.3.refs_3_, bf16[128,256]{1,0:T(8,128)(2,1)S(1)} %copy-done, bf16[128,256]{1,0:T(8,128)(2,1)S(1)} %copy-done.1), custom_call_target="tpu_custom_call" | custom-call | tf_op jit(solution)/shard_map/select/pallas_call | solution.py:55
  16.0 0.7 %collective-permute-start.6 = (f32[1,5120]{1,0:T(1,128)S(1)}, f32[1,5120]{1,0:T(1,128)S(1)}, u32[]{:S(2)}, u32[]{:S(2)}) collective-permute-start(f32[1,5120]{1,0:T(1,128)S(1)} %bitcast.11), channel_id=1, source_target_pairs={{0,1},{1,0},{2,3},{3,2},{4,5},{5,4},{6,7},{7,6},{8,9},{9,8},{10,11... | collective-permute-start | bytes 61448 | tf_op jit(solution)/shard_map/ppermute | solution.py:77
  16.7 0.6 %sub.7 = f32[40,128]{1,0:T(8,128)} subtract(f32[40,128]{1,0:T(8,128)S(1)} %get-tuple-element.13, f32[40,128]{1,0:T(8,128)S(1)} %get-tuple-element.12) | non-fusion elementwise | flops 5120 | bytes 61440 | tf_op jit(solution)/shard_map/sub | solution.py:156
  17.3 0.2 %collective-permute-done.6 = f32[1,5120]{1,0:T(1,128)S(1)} collective-permute-done((f32[1,5120]{1,0:T(1,128)S(1)}, f32[1,5120]{1,0:T(1,128)S(1)}, u32[]{:S(2)}, u32[]{:S(2)}) %collective-permute-start.6) | collective-permute-done | bytes 20512 | tf_op jit(solution)/shard_map/ppermute | solution.py:77
  17.6 0.0 copy-done.3
  17.6 0.6 %multiply_subtract_fusion = f32[1,5120]{1,0:T(1,128)} fusion(f32[1,5120]{1,0:T(1,128)S(1)} %copy-done.3, f32[1,5120]{1,0:T(1,128)S(1)} %bitcast.12, f32[1,5120]{1,0:T(1,128)S(1)} %collective-permute-done.6), kind=kLoop, calls=%fused_computation.3 | loop fusion | flops 15360 | bytes 81920 | tf_op jit(solution)/shard_map/sub | solution.py:156
  (3 shorter events, 0.1 us)
Async XLA Ops:
  0.6 15.1 %copy-start = (bf16[128,256]{1,0:T(8,128)(2,1)S(1)}, bf16[128,256]{1,0:T(8,128)(2,1)}, u32[]{:S(2)}) copy-start(bf16[128,256]{1,0:T(8,128)(2,1)} %constant.14.clone.refs_4_) | copy-start | bytes 196612
  0.6 15.1 %copy-start.1 = (bf16[128,256]{1,0:T(8,128)(2,1)S(1)}, bf16[128,256]{1,0:T(8,128)(2,1)}, u32[]{:S(2)}) copy-start(bf16[128,256]{1,0:T(8,128)(2,1)} %constant.15.clone.refs_5_) | copy-start | bytes 196612
  0.7 8.0 %copy-start.4 = (s32[1,1,40,16]{2,3,1,0:T(8,128)S(1)}, s32[1,1,40,16]{2,3,1,0:T(8,128)}, u32[]{:S(2)}) copy-start(s32[1,1,40,16]{2,3,1,0:T(8,128)} %param.11) | copy-start | bytes 7684
  0.7 15.1 %copy-start.2 = (f32[1,1,5120]{2,1,0:T(1,128)S(1)}, f32[1,1,5120]{2,1,0:T(1,128)}, u32[]{:S(2)}) copy-start(f32[1,1,5120]{2,1,0:T(1,128)} %param.10) | copy-start | bytes 61444
  0.7 16.9 %copy-start.3 = (f32[1,5120]{1,0:T(1,128)S(1)}, f32[1,5120]{1,0:T(1,128)}, u32[]{:S(2)}) copy-start(f32[1,5120]{1,0:T(1,128)} %param.9) | copy-start | bytes 61444
  2.7 6.0 %collective-permute-start = (f32[2,5120]{1,0:T(2,128)S(1)}, f32[2,5120]{1,0:T(2,128)S(1)}, u32[]{:S(2)}, u32[]{:S(2)}) collective-permute-start(f32[2,5120]{1,0:T(2,128)S(1)} %get-tuple-element.8), channel_id=1, source_target_pairs={{0,1},{1,0},{2,3},{3,2},{4,5},{5,4},{6,7},{7,6},{8,9},{9,8},{10,11... | collective-permute-start | bytes 122888 | tf_op jit(solution)/shard_map/ppermute | solution.py:77
  3.3 5.4 %collective-permute-start.1 = (f32[2,5120]{1,0:T(2,128)S(1)}, f32[2,5120]{1,0:T(2,128)S(1)}, u32[]{:S(2)}, u32[]{:S(2)}) collective-permute-start(f32[2,5120]{1,0:T(2,128)S(1)} %get-tuple-element.9), channel_id=1, source_target_pairs={{0,3},{1,2},{2,7},{3,6},{4,1},{5,0},{6,5},{7,4},{8,11},{9,10},{10,... | collective-permute-start | bytes 122888 | tf_op jit(solution)/shard_map/ppermute | solution.py:77
  5.9 3.6 %collective-permute-start.2 = (f32[2,5120]{1,0:T(2,128)S(1)}, f32[2,5120]{1,0:T(2,128)S(1)}, u32[]{:S(2)}, u32[]{:S(2)}) collective-permute-start(f32[2,5120]{1,0:T(2,128)S(1)} %get-tuple-element.10), channel_id=1, source_target_pairs={{0,5},{1,4},{2,1},{3,0},{4,7},{5,6},{6,3},{7,2},{8,13},{9,12},{10,... | collective-permute-start | bytes 122888 | tf_op jit(solution)/shard_map/ppermute | solution.py:77
  6.0 5.4 %collective-permute-start.3 = (f32[2,5120]{1,0:T(2,128)S(1)}, f32[2,5120]{1,0:T(2,128)S(1)}, u32[]{:S(2)}, u32[]{:S(2)}) collective-permute-start(f32[2,5120]{1,0:T(2,128)S(1)} %get-tuple-element.11), channel_id=1, source_target_pairs={{0,7},{1,6},{2,5},{3,4},{4,3},{5,2},{6,1},{7,0},{8,15},{9,14},{10,... | collective-permute-start | bytes 122888 | tf_op jit(solution)/shard_map/ppermute | solution.py:77
  11.5 3.0 %collective-permute-start.4 = (f32[1,5120]{1,0:T(1,128)S(1)}, f32[1,5120]{1,0:T(1,128)S(1)}, u32[]{:S(2)}, u32[]{:S(2)}) collective-permute-start(f32[1,5120]{1,0:T(1,128)S(1)} %get-tuple-element.15), channel_id=1, source_target_pairs={{0,1},{1,0},{2,3},{3,2},{4,5},{5,4},{6,7},{7,6},{8,9},{9,8},{10,11... | collective-permute-start | bytes 61448 | tf_op jit(solution)/shard_map/ppermute | solution.py:77
  11.6 4.1 %collective-permute-start.5 = (f32[1,5120]{1,0:T(1,128)S(1)}, f32[1,5120]{1,0:T(1,128)S(1)}, u32[]{:S(2)}, u32[]{:S(2)}) collective-permute-start(f32[1,5120]{1,0:T(1,128)S(1)} %get-tuple-element.14), channel_id=1, source_target_pairs={{0,9},{1,8},{2,11},{3,10},{4,13},{5,12},{6,15},{7,14},{8,1},{9,0},... | collective-permute-start | bytes 61448 | tf_op jit(solution)/shard_map/ppermute | solution.py:77
  16.0 1.5 %collective-permute-start.6 = (f32[1,5120]{1,0:T(1,128)S(1)}, f32[1,5120]{1,0:T(1,128)S(1)}, u32[]{:S(2)}, u32[]{:S(2)}) collective-permute-start(f32[1,5120]{1,0:T(1,128)S(1)} %bitcast.11), channel_id=1, source_target_pairs={{0,1},{1,0},{2,3},{3,2},{4,5},{5,4},{6,7},{7,6},{8,9},{9,8},{10,11... | collective-permute-start | bytes 61448 | tf_op jit(solution)/shard_map/ppermute | solution.py:77
